TPU v7x, 512 devices: a whole 4x8x8 slice. The times are simulated.
512 devices in a mesh: pages: 16 (over y, core), row: 8 (over z), col: 4 (over x).
Axes of the slice: x: 4, y: 8, z: 8, core: 2. Of those that a mesh axis runs over, the one named last changes fastest.
Arguments:
- residual: bfloat16 [512, 2, 2048], P('pages', None, ('row', 'col')), may hold values from -6 to 6
- fresh_qkv: bfloat16 [512, 2, 3, 2048], P('pages', None, None, 'col'), may hold values from -27 to 27
- prefix_pages: bfloat16 [256, 2, 128, 2048], P('pages', None, 'row', 'col'), may hold values from -6 to 6
- tail_pages: bfloat16 [512, 2, 128, 2048], P('pages', None, 'row', 'col'), may hold values from -6 to 6
- prefix_item: int32 [256], replicated, may hold values from 0 to 255, as said below
- tail_item: int32 [512], replicated, may hold values from 0 to 511, as said below
- prefix_length: int32 [32], replicated, may hold values from 1 to 1024, 20480 in all
- tail_length: int32 [512], replicated, may hold values from 1 to 128, 40960 in all
- out_weight: bfloat16 [2048, 2048], P('col', 'row'), may hold values from -0.125 to 0.125
- out_bias: bfloat16 [2048], P(('row', 'col')), may hold values from -4 to 4
- mlp_gain: bfloat16 [2048], P('row'), may hold values from 0.25 to 1.75
- mlp_shift: bfloat16 [2048], P('row'), may hold values from -4 to 4
- up_weight: bfloat16 [2048, 8192], P('row', 'col'), may hold values from -0.125 to 0.125
- up_bias: bfloat16 [8192], P(('col', 'row')), may hold values from -4 to 4
- down_weight: bfloat16 [8192, 2048], P('col', 'row'), may hold values from -0.0625 to 0.0625
- down_bias: bfloat16 [2048], P(('row', 'col')), may hold values from -4 to 4
- next_gain: bfloat16 [2048], P('row'), may hold values from 0.25 to 1.75
- next_shift: bfloat16 [2048], P('row'), may hold values from -4 to 4
- score_weight: bfloat16 [2048], P('row'), may hold values from -0.125 to 0.125
- qkv_weight: bfloat16 [2048, 6144], P('row', 'col'), may hold values from -0.125 to 0.125
- qkv_bias: bfloat16 [6144], P(('col', 'row')), may hold values from -4 to 4
Outputs:
- layer_out: bfloat16 [512, 2, 2048], P('pages', None, ('row', 'col'))
- score_out: float32 [512, 2], P('pages')
- projected_next: bfloat16 [512, 2, 6144], P('pages', None, ('col', 'row'))
Inputs may be any that keep to these rules, and one draw needn't show every extreme that they name: `prefix_item`: each of the 256 prompt pages is held by exactly one slot; slot h * 16 + g + k (k < 1) holds a page of one of the prompts g * 2 to (g + 1) * 2 - 1. `tail_item`: each continuation's tail is held by exactly one slot; slot h * 32 + g * 2 + k (k < 2) holds the tail of one of the continuations g * 32 to (g + 1) * 32 - 1. `prefix_length`: some prompt has exactly 1024 cached tokens. `tail_length`: some continuation has exactly 128 tail tokens.
All inputs are finite; a program needn't handle non-finite values.
Results may differ from a plain program's by a relative error of at most 0.023.
Values may be sent and summed in bfloat16 or wider, within the bound.
No kernel may reach another device: no remote copies, remote signals or barrier semaphores. Data moves between devices by JAX's collectives and lax.ppermute only.
A program may use at most 64 MiB of HBM per device.

v0:
```python
import math
import jax
import jax.numpy as jnp
from jax import lax
from jax.sharding import PartitionSpec as P

D = 2048
H = 16
HD = 128
PAGE = 128
MAXPAGES = 8
CONT = 16
masked_score = -1e30
norm_eps = 1e-05


def combined_all(shard, axis, combine):
    everything = jax.tree.map(lambda part: lax.all_gather(part, axis), shard)
    first = jax.tree.map(lambda part: part[0], everything)

    def step(k, so_far):
        return combine(so_far, jax.tree.map(lambda part: part[k], everything))

    return lax.fori_loop(1, lax.axis_size(axis), step, first)


def head_slopes(first_head, how_many):
    head_index = first_head + jnp.arange(how_many, dtype=jnp.int32)
    return jnp.exp2(-8.0 * (head_index + 1).astype(jnp.float32) / H)


def slot_partials(queries, page_keys, page_values, usable, offset, slopes):
    scores = jnp.einsum(
        "sqhd,skhd->sqhk", queries, page_keys, preferred_element_type=jnp.float32
    ) / math.sqrt(HD)
    scores = scores + slopes[None, None, :, None] * offset[:, :, None, :]
    usable_full = usable[:, :, None, :]
    scores = jnp.where(usable_full, scores, masked_score)
    maxima = jnp.max(scores, axis=3)
    weights = jnp.where(usable_full, jnp.exp(scores - maxima[..., None]), 0.0)
    totals = jnp.sum(weights, axis=3)
    outputs = jnp.einsum(
        "sqhk,skhd->sqhd", weights, page_values.astype(jnp.float32), precision=lax.Precision.HIGHEST
    )
    return (maxima, totals, outputs)


def merge_pair(left_part, right_part):
    left_max, left_total, left_out = left_part
    right_max, right_total, right_out = right_part
    joined = jnp.maximum(left_max, right_max)
    left_scale = jnp.exp(left_max - joined)
    right_scale = jnp.exp(right_max - joined)
    return (
        joined,
        left_scale * left_total + right_scale * right_total,
        left_scale[..., None] * left_out + right_scale[..., None] * right_out,
    )


def fold_sources(maxima, totals, outputs):
    joined = jnp.max(maxima, axis=0)
    rescale = jnp.exp(maxima - joined[None])
    return (
        joined,
        jnp.sum(rescale * totals, axis=0),
        jnp.sum(rescale[..., None] * outputs, axis=0),
    )


def cache_partials(
    queries,
    page_block,
    page_item,
    tail_block,
    tail_owner,
    prefix_length,
    tail_length,
    row_index,
    slopes,
):
    cont_count = queries.shape[0]
    prompts = cont_count // CONT
    head_count = queries.shape[2]
    slot_count = page_block.shape[0]
    tokens = page_block.shape[2]
    token_index = row_index * tokens + jnp.arange(tokens, dtype=jnp.int32)
    step_index = jnp.arange(2, dtype=jnp.int32)
    slot_prompt = page_item // MAXPAGES
    slot_page = page_item % MAXPAGES
    by_prompt = queries.reshape(prompts, CONT * 2, head_count, HD)
    key_pos = slot_page[:, None] * PAGE + token_index[None, :]
    slot_len = prefix_length[slot_prompt]
    slot_tails = tail_length.reshape(prompts, CONT)[slot_prompt]
    query_pos = (
        slot_len[:, None, None] + slot_tails[:, :, None] + step_index[None, None, :]
    ).reshape(slot_count, CONT * 2)
    offset = (key_pos[:, None, :] - query_pos[:, :, None]).astype(jnp.float32)
    usable = jnp.broadcast_to((key_pos < slot_len[:, None])[:, None, :], offset.shape)
    page_keys = page_block[:, 0].reshape(slot_count, tokens, head_count, HD)
    page_values = page_block[:, 1].reshape(slot_count, tokens, head_count, HD)
    maxima, totals, outputs = slot_partials(
        by_prompt[slot_prompt], page_keys, page_values, usable, offset, slopes
    )
    prompt_max = (
        jnp.full((prompts, CONT * 2, head_count), masked_score, jnp.float32)
        .at[slot_prompt]
        .max(maxima)
    )
    rescale = jnp.exp(maxima - prompt_max[slot_prompt])
    prompt_total = (
        jnp.zeros((prompts, CONT * 2, head_count), jnp.float32)
        .at[slot_prompt]
        .add(rescale * totals)
    )
    prompt_out = (
        jnp.zeros((prompts, CONT * 2, head_count, HD), jnp.float32)
        .at[slot_prompt]
        .add(rescale[..., None] * outputs)
    )
    prefix_part = (
        prompt_max.reshape(cont_count, 2, head_count),
        prompt_total.reshape(cont_count, 2, head_count),
        prompt_out.reshape(cont_count, 2, head_count, HD),
    )
    tail_count = tail_block.shape[0]
    tail_lens = tail_length[tail_owner]
    tail_usable = jnp.broadcast_to(
        (token_index[None, :] < tail_lens[:, None])[:, None, :], (tail_count, 2, tokens)
    )
    tail_offset = (
        token_index[None, None, :] - tail_lens[:, None, None] - step_index[None, :, None]
    ).astype(jnp.float32)
    tail_keys = tail_block[:, 0].reshape(tail_count, tokens, head_count, HD)
    tail_values = tail_block[:, 1].reshape(tail_count, tokens, head_count, HD)
    tail_max, tail_total, tail_out = slot_partials(
        queries[tail_owner], tail_keys, tail_values, tail_usable, tail_offset, slopes
    )
    cont_max = (
        jnp.full((cont_count, 2, head_count), masked_score, jnp.float32)
        .at[tail_owner]
        .set(tail_max)
    )
    cont_total = jnp.zeros((cont_count, 2, head_count), jnp.float32).at[tail_owner].set(tail_total)
    cont_out = jnp.zeros((cont_count, 2, head_count, HD), jnp.float32).at[tail_owner].set(tail_out)
    return merge_pair(prefix_part, (cont_max, cont_total, cont_out))


def normalize(values, sum_one, sum_two, gain, shift):
    center = sum_one / D
    spread = sum_two / D - center * center
    return (
        (values - center[:, None])
        * lax.rsqrt(spread + norm_eps)[:, None]
        * gain.astype(jnp.float32)
        + shift.astype(jnp.float32)
    ).astype(jnp.bfloat16)


def shards(
    residual,
    fresh_qkv,
    prefix_pages,
    tail_pages,
    prefix_item,
    tail_item,
    prefix_length,
    tail_length,
    out_weight,
    out_bias,
    mlp_gain,
    mlp_shift,
    up_weight,
    up_bias,
    down_weight,
    down_bias,
    next_gain,
    next_shift,
    score_weight,
    qkv_weight,
    qkv_bias,
):
    group_index = lax.axis_index("pages")
    row_index = lax.axis_index("row")
    col_index = lax.axis_index("col")
    group_count = lax.axis_size("pages")
    cont_local = residual.shape[0]
    row_total = cont_local * 2
    share = residual.shape[2]
    head_count = fresh_qkv.shape[3] // HD
    slopes = head_slopes(col_index * head_count, head_count)
    fresh_rows = fresh_qkv.reshape(cont_local, 2, 3, head_count, HD)
    slot_count = prefix_pages.shape[0]
    tail_slots = tail_pages.shape[0]
    everyone = lax.all_gather(fresh_qkv[:, :, 0], "pages", axis=0, tiled=True)
    page_item = lax.dynamic_slice_in_dim(prefix_item, group_index * slot_count, slot_count)
    tail_owner = lax.dynamic_slice_in_dim(tail_item, group_index * tail_slots, tail_slots)
    maxima, totals, outputs = cache_partials(
        everyone.reshape(everyone.shape[0], 2, head_count, HD),
        prefix_pages,
        page_item,
        tail_pages,
        tail_owner,
        prefix_length,
        tail_length,
        row_index,
        slopes,
    )
    maxima, totals, outputs = (
        lax.all_to_all(
            maxima.reshape(group_count, row_total, head_count),
            "pages",
            split_axis=0,
            concat_axis=0,
            tiled=True,
        ),
        lax.all_to_all(
            totals.reshape(group_count, row_total, head_count),
            "pages",
            split_axis=0,
            concat_axis=0,
            tiled=True,
        ),
        lax.all_to_all(
            outputs.reshape(group_count, row_total, head_count, HD),
            "pages",
            split_axis=0,
            concat_axis=0,
            tiled=True,
        ),
    )
    cache_max, cache_total, cache_out = fold_sources(maxima, totals, outputs)
    cache_max, cache_total, cache_out = combined_all(
        (cache_max, cache_total, cache_out), "row", merge_pair
    )
    step_index = jnp.arange(2, dtype=jnp.int32)
    new_usable = jnp.broadcast_to(
        (step_index[None, :] <= step_index[:, None])[None], (cont_local, 2, 2)
    )
    new_offset = jnp.broadcast_to(
        (step_index[None, :] - step_index[:, None]).astype(jnp.float32)[None], (cont_local, 2, 2)
    )
    new_part = slot_partials(
        fresh_rows[:, :, 0],
        fresh_rows[:, :, 1],
        fresh_rows[:, :, 2],
        new_usable,
        new_offset,
        slopes,
    )
    joined_max, joined_total, joined_out = merge_pair(
        (
            cache_max.reshape(cont_local, 2, head_count),
            cache_total.reshape(cont_local, 2, head_count),
            cache_out.reshape(cont_local, 2, head_count, HD),
        ),
        new_part,
    )
    attended = (
        (joined_out / joined_total[..., None])
        .astype(jnp.bfloat16)
        .reshape(row_total, head_count * HD)
    )
    head_term = jnp.dot(attended, out_weight, preferred_element_type=jnp.float32)
    hidden_one = (
        residual.reshape(row_total, share).astype(jnp.float32)
        + lax.psum_scatter(head_term, "col", scatter_dimension=1, tiled=True)
        + out_bias.astype(jnp.float32)
    )
    gain_part = lax.dynamic_slice_in_dim(mlp_gain, col_index * share, share)
    shift_part = lax.dynamic_slice_in_dim(mlp_shift, col_index * share, share)
    sum_one, sum_two = lax.psum(
        (jnp.sum(hidden_one, axis=1), jnp.sum(hidden_one * hidden_one, axis=1)), ("row", "col")
    )
    normed_a = lax.all_gather(
        normalize(hidden_one, sum_one, sum_two, gain_part, shift_part), "col", axis=1, tiled=True
    )
    up_share = lax.psum_scatter(
        jnp.dot(normed_a, up_weight, preferred_element_type=jnp.float32),
        "row",
        scatter_dimension=1,
        tiled=True,
    )
    hidden_two = jax.nn.gelu(up_share + up_bias.astype(jnp.float32), approximate=True).astype(
        jnp.bfloat16
    )
    down_sum = jnp.dot(
        lax.all_gather(hidden_two, "row", axis=1, tiled=True),
        down_weight,
        preferred_element_type=jnp.float32,
    )
    down_share = lax.psum_scatter(
        down_sum.astype(jnp.bfloat16), "col", scatter_dimension=1, tiled=True
    ).astype(jnp.float32)
    layer_out = (hidden_one + down_share + down_bias.astype(jnp.float32)).astype(jnp.bfloat16)
    out_wide = layer_out.astype(jnp.float32)
    gain_part = lax.dynamic_slice_in_dim(next_gain, col_index * share, share)
    shift_part = lax.dynamic_slice_in_dim(next_shift, col_index * share, share)
    score_part = lax.dynamic_slice_in_dim(score_weight, col_index * share, share).astype(
        jnp.float32
    )
    sum_one, sum_two, score_sum = lax.psum(
        (
            jnp.sum(out_wide, axis=1),
            jnp.sum(out_wide * out_wide, axis=1),
            jnp.sum(out_wide * score_part, axis=1),
        ),
        ("row", "col"),
    )
    normed_b = lax.all_gather(
        normalize(out_wide, sum_one, sum_two, gain_part, shift_part), "col", axis=1, tiled=True
    )
    qkv_share = lax.psum_scatter(
        jnp.dot(normed_b, qkv_weight, preferred_element_type=jnp.float32).astype(jnp.bfloat16),
        "row",
        scatter_dimension=1,
        tiled=True,
    ).astype(jnp.float32)
    projected_next = (qkv_share + qkv_bias.astype(jnp.float32)).astype(jnp.bfloat16)
    return (
        layer_out.reshape(cont_local, 2, share),
        score_sum.reshape(cont_local, 2),
        projected_next.reshape(cont_local, 2, qkv_share.shape[1]),
    )


def solution(mesh):
    in_specs = (
        P("pages", None, ("row", "col")),
        P("pages", None, None, "col"),
        P("pages", None, "row", "col"),
        P("pages", None, "row", "col"),
        P(),
        P(),
        P(),
        P(),
        P("col", "row"),
        P(("row", "col")),
        P("row"),
        P("row"),
        P("row", "col"),
        P(("col", "row")),
        P("col", "row"),
        P(("row", "col")),
        P("row"),
        P("row"),
        P("row"),
        P("row", "col"),
        P(("col", "row")),
    )
    out_specs = (
        P("pages", None, ("row", "col")),
        P("pages", None),
        P("pages", None, ("col", "row")),
    )
    return jax.shard_map(shards, mesh=mesh, in_specs=in_specs, out_specs=out_specs, check_vma=False)
```

profile of v0, /device:TPU:2, one launch (start us, length us, event | category | flops | bytes accessed | tf_op | source)
XLA Modules:
  0.0 629.2 jit_solution(3406723916201025579)
XLA Ops:
  7.2 1.6 slice.33
  19.9 35.8 %all-gather.9.cloned.1.call-done = bf16[512,2,1,512]{3,1,2,0:T(2,128)(2,1)} async-done(((bf16[32,2,1,512]{3,1,2,0:T(2,128)(2,1)}), bf16[512,2,1,512]{3,1,2,0:T(2,128)(2,1)}) %all-gather.9.cloned.1.call-update) | async-done | bytes 1048592 | tf_op jit(solution)/shard_map/all_gather | solution.py:195
  55.7 1.7 reshape_reshape.3
  59.1 1.5 fusion.61
  62.6 1.5 reshape.233
  64.1 2.0 gather_fusion.4
  66.1 1.6 fusion.60
  72.5 1.5 scatter_fusion.3
  75.7 2.5 multiply_add_fusion
  80.2 4.6 all-to-all-start
  84.8 2.9 fusion.4
  89.6 2.6 scatter_fusion.4
  92.3 1.5 copy.158
  94.5 1.5 scatter_fusion.5
  96.0 7.2 %all-to-all-start.1 = ((f32[16,1,256]{2,1,0:T(1,128)}), f32[16,1,256]{2,1,0:T(1,128)S(1)}, u32[]{:S(2)}, u32[]{:S(2)}) async-start(f32[16,1,256]{2,1,0:T(1,128)} %reshape.385), calls=%async_computation.1 | async-start | bytes 32768 | tf_op jit(solution)/shard_map/all_to_all | solution.py:217
  103.2 6.1 fusion.3
  109.3 1.5 all-to-all-done.1
  110.8 5.7 all-to-all-start.2
  119.8 45.9 %all-to-all-done.2 = f32[16,64,4,128]{3,2,1,0:T(4,128)S(1)} async-done(((f32[16,64,4,128]{3,2,1,0:T(4,128)}), f32[16,64,4,128]{3,2,1,0:T(4,128)S(1)}, u32[]{:S(2)}, u32[]{:S(2)}) %all-to-all-start.2) | async-done | bytes 2097184 | tf_op jit(solution)/shard_map/all_to_all | solution.py:224
  165.7 2.9 multiply_reduce_fusion
  170.9 24.3 %all-gather.4 = f32[8,64,4]{1,2,0:T(4,128)S(1)} all-gather(f32[1,64,4]{1,2,0:T(4,128)S(1)} %copy.149), channel_id=3, replica_groups=mesh['pages'=16,'row'=8,'col'=4] {'row'}, dimensions={0}, use_global_device_ids=true | all-gather | bytes 9216 | tf_op jit(solution)/shard_map/all_gather | solution.py:18
  195.2 21.2 %all-gather.5 = f32[8,64,4]{1,2,0:T(4,128)S(1)} all-gather(f32[1,64,4]{1,2,0:T(4,128)S(1)} %copy.155), channel_id=4, replica_groups=mesh['pages'=16,'row'=8,'col'=4] {'row'}, dimensions={0}, use_global_device_ids=true | all-gather | bytes 9216 | tf_op jit(solution)/shard_map/all_gather | solution.py:18
  217.3 10.9 %while.19 = (s32[]{:T(128)}, f32[64,4]{0,1:T(4,128)S(1)}, f32[64,4]{0,1:T(4,128)S(1)}, f32[64,4,128]{2,1,0:T(4,128)S(1)}, f32[8,64,4]{1,2,0:T(4,128)S(1)}, /*ind...) while((s32[]{:T(128)}, f32[64,4]{0,1:T(4,128)S(1)}, ...), condition=%wide.region_14.15_spmd, body=%wide.region_13.14_spmd.sunk | while | flops 99845 | bytes 407703 | solution.py:24
  230.1 20.7 %reduce-scatter.13.cloned.1.call-done = f32[64,64]{1,0:T(8,128)} async-done(((f32[256,64]{1,0:T(8,128)}), f32[64,64]{1,0:T(8,128)}) %reduce-scatter.13.cloned.1.call-update) | async-done | bytes 16400
  251.7 71.3 %all-reduce.1 = (f32[64]{0:T(128)S(1)}, f32[64]{0:T(128)S(1)}) all-reduce(f32[64]{0:T(128)S(1)} %get-tuple-element.200, f32[64]{0:T(128)S(1)} %get-tuple-element.199), channel_id=1, replica_groups=mesh['pages'=16,'row'=8,'col'=4] {'row','col'}, use_global_device_ids=true, to_apply=%region_21.22 | all-reduce | flops 128 | bytes 1024 | tf_op jit(solution)/shard_map/psum | solution.py:272
  323.2 12.8 %all_gather.37 = bf16[64,256]{0,1:T(8,128)(2,1)S(1)} all-gather(bf16[64,64]{0,1:T(8,128)(2,1)S(1)} %copy.179), channel_id=1, replica_groups=mesh['pages'=16,'row'=8,'col'=4] {'col'}, dimensions={1}, use_global_device_ids=true | all-gather | bytes 40960 | tf_op jit(solution)/shard_map/all_gather | solution.py:275
  337.4 39.7 %reduce-scatter.11.cloned.1.call-done = f32[64,256]{1,0:T(8,128)} async-done(((f32[64,2048]{1,0:T(8,128)}), f32[64,256]{1,0:T(8,128)}) %reduce-scatter.11.cloned.1.call-update) | async-done | bytes 65552 | tf_op jit(solution)/shard_map/reduce_scatter | solution.py:278
  378.0 24.8 %all_gather.38 = bf16[64,2048]{1,0:T(8,128)(2,1)S(1)} all-gather(bf16[64,256]{1,0:T(8,128)(2,1)S(1)} %fusion.32), channel_id=1, replica_groups=mesh['pages'=16,'row'=8,'col'=4] {'row'}, dimensions={1}, use_global_device_ids=true | all-gather | bytes 294912 | tf_op jit(solution)/shard_map/all_gather | solution.py:288
  403.9 22.6 %reduce-scatter.15.cloned.1.call-done = bf16[64,64]{1,0:T(8,128)(2,1)} async-done(((bf16[256,64]{1,0:T(8,128)(2,1)}), bf16[64,64]{1,0:T(8,128)(2,1)}) %reduce-scatter.15.cloned.1.call-update) | async-done | bytes 8208
  427.6 138.0 %all-reduce = (f32[32,2]{1,0:T(8,128)S(1)}, f32[64]{0:T(128)S(1)}, f32[64]{0:T(128)S(1)}) all-reduce(f32[32,2]{1,0:T(8,128)S(1)} %reshape.245, f32[64]{0:T(128)S(1)} %get-tuple-element.202, f32[64]{0:T(128)S(1)} %get-tuple-element.201), channel_id=1, replica_groups=mesh['pages'=16,'row'=8,'col'=4] {'row','col'}, use_global_device_ids=true, to_apply=%region_25.26 | all-reduce | flops 192 | bytes 1536 | tf_op jit(solution)/shard_map/psum | solution.py:302
  565.8 14.2 %all_gather.39 = bf16[64,256]{0,1:T(8,128)(2,1)S(1)} all-gather(bf16[64,64]{0,1:T(8,128)(2,1)S(1)} %copy.180), channel_id=1, replica_groups=mesh['pages'=16,'row'=8,'col'=4] {'col'}, dimensions={1}, use_global_device_ids=true | all-gather | bytes 40960 | tf_op jit(solution)/shard_map/all_gather | solution.py:310
  581.9 38.9 %reduce-scatter.17.cloned.1.call-done = bf16[192,64]{1,0:T(8,128)(2,1)} async-done(((bf16[1536,64]{1,0:T(8,128)(2,1)}), bf16[192,64]{1,0:T(8,128)(2,1)}) %reduce-scatter.17.cloned.1.call-update) | async-done | bytes 24592
  (229 shorter events, 53.5 us)
Async XLA Ops:
  7.2 328.9 %copy-start = (bf16[256,2048]{1,0:T(8,128)(2,1)S(1)}, bf16[256,2048]{1,0:T(8,128)(2,1)}, u32[]{:S(2)}) copy-start(bf16[256,2048]{1,0:T(8,128)(2,1)} %param.35) | copy-start | bytes 3145732
  7.2 48.5 %all-gather.9.cloned.1.call-start = ((), (), s32[]{:S(2)}) async-start(), calls=%async_computation.8 | async-start | bytes 1114112 | tf_op jit(solution)/shard_map/all_gather | solution.py:195
  14.8 55.5 %copy-start.19 = (s32[16]{0:T(128)}, s32[16]{0:T(128)S(1)}, u32[]{:S(2)}) copy-start(s32[16]{0:T(128)S(1)} %compare_select_fusion.1) | copy-start | bytes 196
  18.9 50.4 %copy-start.16 = (pred[16,16]{1,0:T(8,128)(4,1)}, pred[16,16]{1,0:T(8,128)(4,1)S(1)}, u32[]{:S(2)}) copy-start(pred[16,16]{1,0:T(8,128)(4,1)S(1)} %broadcast_compare_fusion.1) | copy-start | bytes 772
  19.0 49.6 %copy-start.17 = (pred[32,16]{1,0:T(8,128)(4,1)}, pred[32,16]{1,0:T(8,128)(4,1)S(1)}, u32[]{:S(2)}) copy-start(pred[32,16]{1,0:T(8,128)(4,1)S(1)} %broadcast_compare_fusion) | copy-start | bytes 1540
  78.2 9.5 %copy-start.7 = (bf16[32,16,4,128]{3,2,1,0:T(4,128)(2,1)S(1)}, bf16[32,16,4,128]{3,2,1,0:T(4,128)(2,1)}, u32[]{:S(2)}) copy-start(bf16[32,16,4,128]{3,2,1,0:T(4,128)(2,1)} %reshape_squeeze.15) | copy-start | bytes 1572868
  78.2 9.5 %copy-start.14 = (f32[32,2,4,16]{3,1,2,0:T(2,128)S(1)}, f32[32,2,4,16]{3,1,2,0:T(2,128)}, u32[]{:S(2)}) copy-start(f32[32,2,4,16]{3,1,2,0:T(2,128)} %copy-done.13) | copy-start | bytes 49156
  78.2 9.5 %copy-start.18 = (pred[32,16]{1,0:T(8,128)(4,1)S(1)}, pred[32,16]{1,0:T(8,128)(4,1)}, u32[]{:S(2)}) copy-start(pred[32,16]{1,0:T(8,128)(4,1)} %copy-done.17) | copy-start | bytes 1540
  80.2 15.7 %all-to-all-start = ((f32[16,1,256]{2,1,0:T(1,128)}), f32[16,1,256]{2,1,0:T(1,128)S(1)}, u32[]{:S(2)}, u32[]{:S(2)}) async-start(f32[16,1,256]{2,1,0:T(1,128)} %reshape.383), calls=%async_computation | async-start | bytes 32768 | tf_op jit(solution)/shard_map/all_to_all | solution.py:210
  96.0 14.9 %all-to-all-start.1 = ((f32[16,1,256]{2,1,0:T(1,128)}), f32[16,1,256]{2,1,0:T(1,128)S(1)}, u32[]{:S(2)}, u32[]{:S(2)}) async-start(f32[16,1,256]{2,1,0:T(1,128)} %reshape.385), calls=%async_computation.1 | async-start | bytes 32768 | tf_op jit(solution)/shard_map/all_to_all | solution.py:217
  110.8 54.9 %all-to-all-start.2 = ((f32[16,64,4,128]{3,2,1,0:T(4,128)}), f32[16,64,4,128]{3,2,1,0:T(4,128)S(1)}, u32[]{:S(2)}, u32[]{:S(2)}) async-start(f32[16,64,4,128]{3,2,1,0:T(4,128)} %bitcast.145), calls=%async_computation.2 | async-start | bytes 4194304 | tf_op jit(solution)/shard_map/all_to_all | solution.py:224
  116.5 52.1 %copy-start.8 = (bf16[32,2,3,512]{3,1,2,0:T(2,128)(2,1)S(1)}, bf16[32,2,3,512]{3,1,2,0:T(2,128)(2,1)}, u32[]{:S(2)}) copy-start(bf16[32,2,3,512]{3,1,2,0:T(2,128)(2,1)} %param.24) | copy-start | bytes 589828
  116.5 99.8 %all-gather.11.cloned.1.call-start = ((), (), s32[]{:S(2)}) async-start(), calls=%async_computation.9 | async-start | bytes 1179648 | tf_op jit(solution)/shard_map/all_gather | solution.py:18
  118.7 50.2 %copy-start.35 = (f32[4]{0:T(128)S(1)}, f32[4]{0:T(128)}, u32[]{:S(2)}) copy-start(f32[4]{0:T(128)} %multiply_exponential_fusion) | copy-start | bytes 52
  168.6 82.1 %reduce-scatter.13.cloned.1.call-start = ((), (), s32[]{:S(2)}) async-start(), calls=%async_computation.10 | async-start | bytes 163840
  170.5 58.4 %copy-start.9 = (bf16[512,256]{1,0:T(8,128)(2,1)S(1)}, bf16[512,256]{1,0:T(8,128)(2,1)}, u32[]{:S(2)}) copy-start(bf16[512,256]{1,0:T(8,128)(2,1)} %param.31) | copy-start | bytes 786436
  217.3 12.7 %copy-start.30 = (bf16[64]{0:T(256)(128)(2,1)S(1)}, bf16[64]{0:T(256)(128)(2,1)}, u32[]{:S(2)}) copy-start(bf16[64]{0:T(256)(128)(2,1)} %param.32) | copy-start | bytes 388
  217.3 12.7 %copy-start.26 = (bf16[256]{0:T(256)(128)(2,1)S(1)}, bf16[256]{0:T(256)(128)(2,1)}, u32[]{:S(2)}) copy-start(bf16[256]{0:T(256)(128)(2,1)} %param.34) | copy-start | bytes 1540
  217.3 12.7 %copy-start.27 = (bf16[256]{0:T(256)(128)(2,1)S(1)}, bf16[256]{0:T(256)(128)(2,1)}, u32[]{:S(2)}) copy-start(bf16[256]{0:T(256)(128)(2,1)} %param.33) | copy-start | bytes 1540
  217.3 34.3 %copy-start.10 = (bf16[32,2,64]{2,1,0:T(2,128)(2,1)S(1)}, bf16[32,2,64]{2,1,0:T(2,128)(2,1)}, u32[]{:S(2)}) copy-start(bf16[32,2,64]{2,1,0:T(2,128)(2,1)} %param.23) | copy-start | bytes 24580
  228.3 109.0 %copy-start.31 = (bf16[64]{0:T(256)(128)(2,1)S(1)}, bf16[64]{0:T(256)(128)(2,1)}, u32[]{:S(2)}) copy-start(bf16[64]{0:T(256)(128)(2,1)} %param.38) | copy-start | bytes 388
  228.3 109.0 %copy-start.32 = (bf16[256]{0:T(256)(128)(2,1)S(1)}, bf16[256]{0:T(256)(128)(2,1)}, u32[]{:S(2)}) copy-start(bf16[256]{0:T(256)(128)(2,1)} %param.36) | copy-start | bytes 1540
  228.3 109.0 %copy-start.28 = (bf16[256]{0:T(256)(128)(2,1)S(1)}, bf16[256]{0:T(256)(128)(2,1)}, u32[]{:S(2)}) copy-start(bf16[256]{0:T(256)(128)(2,1)} %param.40) | copy-start | bytes 1540
  228.3 109.0 %copy-start.29 = (bf16[256]{0:T(256)(128)(2,1)S(1)}, bf16[256]{0:T(256)(128)(2,1)}, u32[]{:S(2)}) copy-start(bf16[256]{0:T(256)(128)(2,1)} %param.39) | copy-start | bytes 1540
  228.3 174.5 %copy-start.4 = (bf16[2048,256]{1,0:T(8,128)(2,1)S(1)}, bf16[2048,256]{1,0:T(8,128)(2,1)}, u32[]{:S(2)}) copy-start(bf16[2048,256]{1,0:T(8,128)(2,1)} %param.37) | copy-start | bytes 3145732
  229.9 147.2 %reduce-scatter.11.cloned.1.call-start = ((), (), s32[]{:S(2)}) async-start(), calls=%async_computation.7 | async-start | bytes 589824 | tf_op jit(solution)/shard_map/reduce_scatter | solution.py:278
  323.1 80.7 %copy-start.33 = (bf16[256]{0:T(256)(128)(2,1)S(1)}, bf16[256]{0:T(256)(128)(2,1)}, u32[]{:S(2)}) copy-start(bf16[256]{0:T(256)(128)(2,1)} %param.41) | copy-start | bytes 1540
  336.1 244.0 %copy-start.5 = (bf16[256,1536]{1,0:T(8,128)(2,1)S(1)}, bf16[256,1536]{1,0:T(8,128)(2,1)}, u32[]{:S(2)}) copy-start(bf16[256,1536]{1,0:T(8,128)(2,1)} %param.42) | copy-start | bytes 2359300
  337.2 89.3 %reduce-scatter.15.cloned.1.call-start = ((), (), s32[]{:S(2)}) async-start(), calls=%async_computation.11 | async-start | bytes 81920
  377.9 203.3 %copy-start.34 = (bf16[192]{0:T(256)(128)(2,1)S(1)}, bf16[192]{0:T(256)(128)(2,1)}, u32[]{:S(2)}) copy-start(bf16[192]{0:T(256)(128)(2,1)} %param.43) | copy-start | bytes 1156
  403.8 217.0 %reduce-scatter.17.cloned.1.call-start = ((), (), s32[]{:S(2)}) async-start(), calls=%async_computation.12 | async-start | bytes 442368
  427.5 194.9 %copy-start.15 = (bf16[64,64]{1,0:T(8,128)(2,1)}, bf16[64,64]{1,0:T(8,128)(2,1)S(1)}, u32[]{:S(2)}) copy-start(bf16[64,64]{1,0:T(8,128)(2,1)S(1)} %get-tuple-element.227) | copy-start | bytes 24580
  (13 other events, 59.2 us)
Sparse Core Ops, SparseCore 0:
  10.2 45.5 all-gather.8
  168.7 41.4 all-gather.10
  230.0 20.6 reduce-scatter.12
  337.3 39.6 reduce-scatter.10
  403.9 22.5 reduce-scatter.14
  581.4 39.4 reduce-scatter.16
where the time goes:
time: 630 us; the launch traced here: 629 us
  blocking collectives  307 us (49%)
  waiting for transfers between devices  205 us (33%)
  local copies, waits for them, and re-layouts  40.9 us (6%)
  other arithmetic  33.2 us (5%)
  starting transfers between devices  17.7 us (3%)
  between operations  14.9 us (2%)
  matrix products  10.4 us (2%)
    psum x1, blocking collectives, shards(): lax.psum((jnp.sum(out_wide, axis=1), jnp.sum(out_wide * out_wide, axis=1)...  138 us
    unnamed x9, waiting for transfers between devices  82.3 us
    psum x1, blocking collectives, shards(): lax.psum((jnp.sum(hidden_one, axis=1), jnp.sum(hidden_one * hidden_one, a...  71.3 us
    all_to_all x1, waiting for transfers between devices, shards(): lax.all_to_all(outputs.reshape(group_count, row_total, head_count, HD), '...  45.9 us
    all_gather x2, blocking collectives, combined_all(): everything = jax.tree.map(lambda part: lax.all_gather(part, axis), shard)  45.5 us
    reduce_scatter x1, waiting for transfers between devices, shards(): lax.psum_scatter(jnp.dot(normed_a, up_weight, preferred_element_type=jnp....  39.7 us
    all_gather x1, waiting for transfers between devices, shards(): everyone = lax.all_gather(fresh_qkv[:, :, 0], 'pages', axis=0, tiled=True)  35.8 us
    all_gather x1, blocking collectives, shards(): lax.all_gather(hidden_two, 'row', axis=1, tiled=True)  24.8 us
  transfers between devices with their start and end apart: 9, of which 7 were waited for; matrix products, arithmetic and copies ran while one was open for 5% of the time, Pallas kernels for 0%

commit v1 on v0

--- a/solution.py
+++ b/solution.py
@@ -300,12 +300,15 @@
         jnp.float32
     )
     sum_one, sum_two, score_sum = lax.psum(
-        (
-            jnp.sum(out_wide, axis=1),
-            jnp.sum(out_wide * out_wide, axis=1),
-            jnp.sum(out_wide * score_part, axis=1),
-        ),
-        ("row", "col"),
+        lax.psum(
+            (
+                jnp.sum(out_wide, axis=1),
+                jnp.sum(out_wide * out_wide, axis=1),
+                jnp.sum(out_wide * score_part, axis=1),
+            ),
+            "row",
+        ),
+        "col",
     )
     normed_b = lax.all_gather(
         normalize(out_wide, sum_one, sum_two, gain_part, shift_part), "col", axis=1, tiled=True

time: 630 us -> 522 us (0.83)
  the two profiles are of different devices: /device:TPU:2 before, /device:TPU:4 now
where the time goes in v1:
time: 522 us; the launch traced here: 521 us
  waiting for transfers between devices  203 us (39%)
  blocking collectives  201 us (39%)
  local copies, waits for them, and re-layouts  40.9 us (8%)
  other arithmetic  33.2 us (6%)
  starting transfers between devices  17.7 us (3%)
  between operations  14.9 us (3%)
  matrix products  10.4 us (2%)
    unnamed x9, waiting for transfers between devices  80.7 us
    psum x1, blocking collectives, shards(): lax.psum((jnp.sum(hidden_one, axis=1), jnp.sum(hidden_one * hidden_one, a...  71.1 us
    all_to_all x1, waiting for transfers between devices, shards(): lax.all_to_all(outputs.reshape(group_count, row_total, head_count, HD), '...  45.9 us
    all_gather x2, blocking collectives, combined_all(): everything = jax.tree.map(lambda part: lax.all_gather(part, axis), shard)  45.5 us
    reduce_scatter x1, waiting for transfers between devices, shards(): lax.psum_scatter(jnp.dot(normed_a, up_weight, preferred_element_type=jnp....  38.5 us
    all_gather x1, waiting for transfers between devices, shards(): everyone = lax.all_gather(fresh_qkv[:, :, 0], 'pages', axis=0, tiled=True)  35.9 us
    all_gather x1, blocking collectives, shards(): lax.all_gather(hidden_two, 'row', axis=1, tiled=True)  24.8 us
    psum x1, blocking collectives, shards(): lax.psum((jnp.sum(out_wide, axis=1), jnp.sum(out_wide * out_wide, axis=1)...  18.1 us
  transfers between devices with their start and end apart: 9, of which 7 were waited for; matrix products, arithmetic and copies ran while one was open for 6% of the time, Pallas kernels for 0%

profile of v1, /device:TPU:4, one launch (start us, length us, event | category | flops | bytes accessed | tf_op | source)
XLA Modules:
  0.0 520.9 jit_solution(8959349826260653352)
XLA Ops:
  7.2 1.6 slice.33
  19.8 35.9 %all-gather.9.cloned.1.call-done = bf16[512,2,1,512]{3,1,2,0:T(2,128)(2,1)} async-done(((bf16[32,2,1,512]{3,1,2,0:T(2,128)(2,1)}), bf16[512,2,1,512]{3,1,2,0:T(2,128)(2,1)}) %all-gather.9.cloned.1.call-update) | async-done | bytes 1048592 | tf_op jit(solution)/shard_map/all_gather | solution.py:195
  55.7 1.7 reshape_reshape.3
  59.1 1.5 fusion.61
  62.6 1.5 reshape.233
  64.1 2.0 gather_fusion.4
  66.1 1.5 fusion.60
  75.6 2.5 multiply_add_fusion
  80.2 4.6 all-to-all-start
  84.8 2.9 fusion.4
  89.6 2.6 scatter_fusion.4
  92.2 1.5 copy.158
  94.4 1.5 scatter_fusion.5
  95.9 7.2 %all-to-all-start.1 = ((f32[16,1,256]{2,1,0:T(1,128)}), f32[16,1,256]{2,1,0:T(1,128)S(1)}, u32[]{:S(2)}, u32[]{:S(2)}) async-start(f32[16,1,256]{2,1,0:T(1,128)} %reshape.385), calls=%async_computation.1 | async-start | bytes 32768 | tf_op jit(solution)/shard_map/all_to_all | solution.py:217
  103.2 6.1 %fusion.3 = f32[512,2,4,128]{3,2,1,0:T(4,128)} fusion(f32[512,2,4,128]{3,1,0,2:T(2,128)} %bitcast.146, f32[512,2,4,128]{3,2,1,0:T(4,128)S(1)} %scatter_fusion.5, f32[512,2,4]{2,1,0:T(2,128)} %bitcast.154, f32[512,2,4]{2,1,0:T(2,128)} %bitcast.153), kind=kLoop, calls=%fused_computation.22 | loop fusion | flops 1572864 | bytes 6324224 | tf_op jit(solution)/shard_map/add | solution.py:57
  109.3 1.5 all-to-all-done.1
  110.8 5.7 %all-to-all-start.2 = ((f32[16,64,4,128]{3,2,1,0:T(4,128)}), f32[16,64,4,128]{3,2,1,0:T(4,128)S(1)}, u32[]{:S(2)}, u32[]{:S(2)}) async-start(f32[16,64,4,128]{3,2,1,0:T(4,128)} %bitcast.145), calls=%async_computation.2 | async-start | bytes 4194304 | tf_op jit(solution)/shard_map/all_to_all | solution.py:224
  119.7 45.9 %all-to-all-done.2 = f32[16,64,4,128]{3,2,1,0:T(4,128)S(1)} async-done(((f32[16,64,4,128]{3,2,1,0:T(4,128)}), f32[16,64,4,128]{3,2,1,0:T(4,128)S(1)}, u32[]{:S(2)}, u32[]{:S(2)}) %all-to-all-start.2) | async-done | bytes 2097184 | tf_op jit(solution)/shard_map/all_to_all | solution.py:224
  165.7 2.9 multiply_reduce_fusion
  170.8 24.3 %all-gather.4 = f32[8,64,4]{1,2,0:T(4,128)S(1)} all-gather(f32[1,64,4]{1,2,0:T(4,128)S(1)} %copy.149), channel_id=3, replica_groups=mesh['pages'=16,'row'=8,'col'=4] {'row'}, dimensions={0}, use_global_device_ids=true | all-gather | bytes 9216 | tf_op jit(solution)/shard_map/all_gather | solution.py:18
  195.1 21.2 %all-gather.5 = f32[8,64,4]{1,2,0:T(4,128)S(1)} all-gather(f32[1,64,4]{1,2,0:T(4,128)S(1)} %copy.155), channel_id=4, replica_groups=mesh['pages'=16,'row'=8,'col'=4] {'row'}, dimensions={0}, use_global_device_ids=true | all-gather | bytes 9216 | tf_op jit(solution)/shard_map/all_gather | solution.py:18
  217.3 10.9 %while.19 = (s32[]{:T(128)}, f32[64,4]{0,1:T(4,128)S(1)}, f32[64,4]{0,1:T(4,128)S(1)}, f32[64,4,128]{2,1,0:T(4,128)S(1)}, f32[8,64,4]{1,2,0:T(4,128)S(1)}, /*ind...) while((s32[]{:T(128)}, f32[64,4]{0,1:T(4,128)S(1)}, ...), condition=%wide.region_14.15_spmd, body=%wide.region_13.14_spmd.sunk | while | flops 99845 | bytes 407703 | solution.py:24
  230.0 20.3 %reduce-scatter.13.cloned.1.call-done = f32[64,64]{1,0:T(8,128)} async-done(((f32[256,64]{1,0:T(8,128)}), f32[64,64]{1,0:T(8,128)}) %reduce-scatter.13.cloned.1.call-update) | async-done | bytes 16400
  251.2 71.1 %all-reduce = (f32[64]{0:T(128)S(1)}, f32[64]{0:T(128)S(1)}) all-reduce(f32[64]{0:T(128)S(1)} %get-tuple-element.200, f32[64]{0:T(128)S(1)} %get-tuple-element.199), channel_id=1, replica_groups=mesh['pages'=16,'row'=8,'col'=4] {'row','col'}, use_global_device_ids=true, to_apply=%region_21.22 | all-reduce | flops 128 | bytes 1024 | tf_op jit(solution)/shard_map/psum | solution.py:272
  322.6 14.6 %all_gather.37 = bf16[64,256]{0,1:T(8,128)(2,1)S(1)} all-gather(bf16[64,64]{0,1:T(8,128)(2,1)S(1)} %copy.179), channel_id=1, replica_groups=mesh['pages'=16,'row'=8,'col'=4] {'col'}, dimensions={1}, use_global_device_ids=true | all-gather | bytes 40960 | tf_op jit(solution)/shard_map/all_gather | solution.py:275
  338.5 38.5 %reduce-scatter.11.cloned.1.call-done = f32[64,256]{1,0:T(8,128)} async-done(((f32[64,2048]{1,0:T(8,128)}), f32[64,256]{1,0:T(8,128)}) %reduce-scatter.11.cloned.1.call-update) | async-done | bytes 65552 | tf_op jit(solution)/shard_map/reduce_scatter | solution.py:278
  377.9 24.8 %all_gather.38 = bf16[64,2048]{1,0:T(8,128)(2,1)S(1)} all-gather(bf16[64,256]{1,0:T(8,128)(2,1)S(1)} %fusion.32), channel_id=1, replica_groups=mesh['pages'=16,'row'=8,'col'=4] {'row'}, dimensions={1}, use_global_device_ids=true | all-gather | bytes 294912 | tf_op jit(solution)/shard_map/all_gather | solution.py:288
  403.8 22.3 %reduce-scatter.15.cloned.1.call-done = bf16[64,64]{1,0:T(8,128)(2,1)} async-done(((bf16[256,64]{1,0:T(8,128)(2,1)}), bf16[64,64]{1,0:T(8,128)(2,1)}) %reduce-scatter.15.cloned.1.call-update) | async-done | bytes 8208
  427.1 18.1 %all-reduce.1 = (f32[64]{0:T(128)S(1)}, f32[64]{0:T(128)S(1)}, f32[64]{0:T(128)S(1)}) all-reduce(f32[64]{0:T(128)S(1)} %get-tuple-element.203, f32[64]{0:T(128)S(1)} %get-tuple-element.202, f32[64]{0:T(128)S(1)} %get-tuple-element.201), channel_id=1, replica_groups=mesh['pages'=16,'row'=8,'col'=4] {'row'}, use_global_device_ids=true, to_apply=%region_25.26 | all-reduce | flops 192 | bytes 1536 | tf_op jit(solution)/shard_map/psum | solution.py:303
  445.3 15.2 %all-reduce.2 = (f32[32,2]{1,0:T(8,128)S(1)}, f32[64]{0:T(128)S(1)}, f32[64]{0:T(128)S(1)}) all-reduce(f32[32,2]{1,0:T(8,128)S(1)} %reshape.245, f32[64]{0:T(128)S(1)} %get-tuple-element.221, f32[64]{0:T(128)S(1)} %get-tuple-element.222), channel_id=1, replica_groups=mesh['pages'=16,'row'=8,'col'=4] {'col'}, use_global_device_ids=true, to_apply=%region_26.27 | all-reduce | flops 192 | bytes 1536 | tf_op jit(solution)/shard_map/psum | solution.py:302
  460.6 11.9 %all_gather.39 = bf16[64,256]{0,1:T(8,128)(2,1)S(1)} all-gather(bf16[64,64]{0,1:T(8,128)(2,1)S(1)} %copy.180), channel_id=1, replica_groups=mesh['pages'=16,'row'=8,'col'=4] {'col'}, dimensions={1}, use_global_device_ids=true | all-gather | bytes 40960 | tf_op jit(solution)/shard_map/all_gather | solution.py:313
  474.4 38.1 %reduce-scatter.17.cloned.1.call-done = bf16[192,64]{1,0:T(8,128)(2,1)} async-done(((bf16[1536,64]{1,0:T(8,128)(2,1)}), bf16[192,64]{1,0:T(8,128)(2,1)}) %reduce-scatter.17.cloned.1.call-update) | async-done | bytes 24592
  (230 shorter events, 54.9 us)
Async XLA Ops:
  7.2 330.0 %copy-start = (bf16[256,2048]{1,0:T(8,128)(2,1)S(1)}, bf16[256,2048]{1,0:T(8,128)(2,1)}, u32[]{:S(2)}) copy-start(bf16[256,2048]{1,0:T(8,128)(2,1)} %param.35) | copy-start | bytes 3145732
  7.2 48.5 %all-gather.9.cloned.1.call-start = ((), (), s32[]{:S(2)}) async-start(), calls=%async_computation.8 | async-start | bytes 1114112 | tf_op jit(solution)/shard_map/all_gather | solution.py:195
  14.7 55.4 %copy-start.19 = (s32[16]{0:T(128)}, s32[16]{0:T(128)S(1)}, u32[]{:S(2)}) copy-start(s32[16]{0:T(128)S(1)} %compare_select_fusion.1) | copy-start | bytes 196
  18.9 50.4 %copy-start.16 = (pred[16,16]{1,0:T(8,128)(4,1)}, pred[16,16]{1,0:T(8,128)(4,1)S(1)}, u32[]{:S(2)}) copy-start(pred[16,16]{1,0:T(8,128)(4,1)S(1)} %broadcast_compare_fusion.1) | copy-start | bytes 772
  18.9 49.6 %copy-start.17 = (pred[32,16]{1,0:T(8,128)(4,1)}, pred[32,16]{1,0:T(8,128)(4,1)S(1)}, u32[]{:S(2)}) copy-start(pred[32,16]{1,0:T(8,128)(4,1)S(1)} %broadcast_compare_fusion) | copy-start | bytes 1540
  78.1 9.6 %copy-start.7 = (bf16[32,16,4,128]{3,2,1,0:T(4,128)(2,1)S(1)}, bf16[32,16,4,128]{3,2,1,0:T(4,128)(2,1)}, u32[]{:S(2)}) copy-start(bf16[32,16,4,128]{3,2,1,0:T(4,128)(2,1)} %reshape_squeeze.15) | copy-start | bytes 1572868
  78.1 9.6 %copy-start.14 = (f32[32,2,4,16]{3,1,2,0:T(2,128)S(1)}, f32[32,2,4,16]{3,1,2,0:T(2,128)}, u32[]{:S(2)}) copy-start(f32[32,2,4,16]{3,1,2,0:T(2,128)} %copy-done.13) | copy-start | bytes 49156
  78.1 9.6 %copy-start.18 = (pred[32,16]{1,0:T(8,128)(4,1)S(1)}, pred[32,16]{1,0:T(8,128)(4,1)}, u32[]{:S(2)}) copy-start(pred[32,16]{1,0:T(8,128)(4,1)} %copy-done.17) | copy-start | bytes 1540
  80.2 15.7 %all-to-all-start = ((f32[16,1,256]{2,1,0:T(1,128)}), f32[16,1,256]{2,1,0:T(1,128)S(1)}, u32[]{:S(2)}, u32[]{:S(2)}) async-start(f32[16,1,256]{2,1,0:T(1,128)} %reshape.383), calls=%async_computation | async-start | bytes 32768 | tf_op jit(solution)/shard_map/all_to_all | solution.py:210
  95.9 14.9 %all-to-all-start.1 = ((f32[16,1,256]{2,1,0:T(1,128)}), f32[16,1,256]{2,1,0:T(1,128)S(1)}, u32[]{:S(2)}, u32[]{:S(2)}) async-start(f32[16,1,256]{2,1,0:T(1,128)} %reshape.385), calls=%async_computation.1 | async-start | bytes 32768 | tf_op jit(solution)/shard_map/all_to_all | solution.py:217
  110.8 54.9 %all-to-all-start.2 = ((f32[16,64,4,128]{3,2,1,0:T(4,128)}), f32[16,64,4,128]{3,2,1,0:T(4,128)S(1)}, u32[]{:S(2)}, u32[]{:S(2)}) async-start(f32[16,64,4,128]{3,2,1,0:T(4,128)} %bitcast.145), calls=%async_computation.2 | async-start | bytes 4194304 | tf_op jit(solution)/shard_map/all_to_all | solution.py:224
  116.5 52.1 %copy-start.8 = (bf16[32,2,3,512]{3,1,2,0:T(2,128)(2,1)S(1)}, bf16[32,2,3,512]{3,1,2,0:T(2,128)(2,1)}, u32[]{:S(2)}) copy-start(bf16[32,2,3,512]{3,1,2,0:T(2,128)(2,1)} %param.24) | copy-start | bytes 589828
  116.5 99.8 %all-gather.11.cloned.1.call-start = ((), (), s32[]{:S(2)}) async-start(), calls=%async_computation.9 | async-start | bytes 1179648 | tf_op jit(solution)/shard_map/all_gather | solution.py:18
  118.7 50.2 %copy-start.35 = (f32[4]{0:T(128)S(1)}, f32[4]{0:T(128)}, u32[]{:S(2)}) copy-start(f32[4]{0:T(128)} %multiply_exponential_fusion) | copy-start | bytes 52
  168.6 81.7 %reduce-scatter.13.cloned.1.call-start = ((), (), s32[]{:S(2)}) async-start(), calls=%async_computation.10 | async-start | bytes 163840
  170.5 58.4 %copy-start.9 = (bf16[512,256]{1,0:T(8,128)(2,1)S(1)}, bf16[512,256]{1,0:T(8,128)(2,1)}, u32[]{:S(2)}) copy-start(bf16[512,256]{1,0:T(8,128)(2,1)} %param.31) | copy-start | bytes 786436
  217.2 12.7 %copy-start.30 = (bf16[64]{0:T(256)(128)(2,1)S(1)}, bf16[64]{0:T(256)(128)(2,1)}, u32[]{:S(2)}) copy-start(bf16[64]{0:T(256)(128)(2,1)} %param.32) | copy-start | bytes 388
  217.2 12.7 %copy-start.26 = (bf16[256]{0:T(256)(128)(2,1)S(1)}, bf16[256]{0:T(256)(128)(2,1)}, u32[]{:S(2)}) copy-start(bf16[256]{0:T(256)(128)(2,1)} %param.34) | copy-start | bytes 1540
  217.3 12.7 %copy-start.27 = (bf16[256]{0:T(256)(128)(2,1)S(1)}, bf16[256]{0:T(256)(128)(2,1)}, u32[]{:S(2)}) copy-start(bf16[256]{0:T(256)(128)(2,1)} %param.33) | copy-start | bytes 1540
  217.3 33.8 %copy-start.10 = (bf16[32,2,64]{2,1,0:T(2,128)(2,1)S(1)}, bf16[32,2,64]{2,1,0:T(2,128)(2,1)}, u32[]{:S(2)}) copy-start(bf16[32,2,64]{2,1,0:T(2,128)(2,1)} %param.23) | copy-start | bytes 24580
  228.2 110.2 %copy-start.31 = (bf16[64]{0:T(256)(128)(2,1)S(1)}, bf16[64]{0:T(256)(128)(2,1)}, u32[]{:S(2)}) copy-start(bf16[64]{0:T(256)(128)(2,1)} %param.38) | copy-start | bytes 388
  228.2 110.2 %copy-start.32 = (bf16[256]{0:T(256)(128)(2,1)S(1)}, bf16[256]{0:T(256)(128)(2,1)}, u32[]{:S(2)}) copy-start(bf16[256]{0:T(256)(128)(2,1)} %param.36) | copy-start | bytes 1540
  228.2 110.2 %copy-start.28 = (bf16[256]{0:T(256)(128)(2,1)S(1)}, bf16[256]{0:T(256)(128)(2,1)}, u32[]{:S(2)}) copy-start(bf16[256]{0:T(256)(128)(2,1)} %param.40) | copy-start | bytes 1540
  228.2 110.2 %copy-start.29 = (bf16[256]{0:T(256)(128)(2,1)S(1)}, bf16[256]{0:T(256)(128)(2,1)}, u32[]{:S(2)}) copy-start(bf16[256]{0:T(256)(128)(2,1)} %param.39) | copy-start | bytes 1540
  228.3 174.4 %copy-start.4 = (bf16[2048,256]{1,0:T(8,128)(2,1)S(1)}, bf16[2048,256]{1,0:T(8,128)(2,1)}, u32[]{:S(2)}) copy-start(bf16[2048,256]{1,0:T(8,128)(2,1)} %param.37) | copy-start | bytes 3145732
  229.8 147.1 %reduce-scatter.11.cloned.1.call-start = ((), (), s32[]{:S(2)}) async-start(), calls=%async_computation.7 | async-start | bytes 589824 | tf_op jit(solution)/shard_map/reduce_scatter | solution.py:278
  322.5 81.3 %copy-start.33 = (bf16[256]{0:T(256)(128)(2,1)S(1)}, bf16[256]{0:T(256)(128)(2,1)}, u32[]{:S(2)}) copy-start(bf16[256]{0:T(256)(128)(2,1)} %param.41) | copy-start | bytes 1540
  337.2 135.3 %copy-start.5 = (bf16[256,1536]{1,0:T(8,128)(2,1)S(1)}, bf16[256,1536]{1,0:T(8,128)(2,1)}, u32[]{:S(2)}) copy-start(bf16[256,1536]{1,0:T(8,128)(2,1)} %param.42) | copy-start | bytes 2359300
  338.3 87.8 %reduce-scatter.15.cloned.1.call-start = ((), (), s32[]{:S(2)}) async-start(), calls=%async_computation.11 | async-start | bytes 81920
  377.8 95.9 %copy-start.34 = (bf16[192]{0:T(256)(128)(2,1)S(1)}, bf16[192]{0:T(256)(128)(2,1)}, u32[]{:S(2)}) copy-start(bf16[192]{0:T(256)(128)(2,1)} %param.43) | copy-start | bytes 1156
  403.7 108.8 %reduce-scatter.17.cloned.1.call-start = ((), (), s32[]{:S(2)}) async-start(), calls=%async_computation.12 | async-start | bytes 442368
  427.1 86.9 %copy-start.15 = (bf16[64,64]{1,0:T(8,128)(2,1)}, bf16[64,64]{1,0:T(8,128)(2,1)S(1)}, u32[]{:S(2)}) copy-start(bf16[64,64]{1,0:T(8,128)(2,1)S(1)} %get-tuple-element.230) | copy-start | bytes 24580
  (13 other events, 59.2 us)
Sparse Core Ops, SparseCore 0:
  10.2 45.4 all-gather.8
  168.7 41.4 all-gather.10
  230.0 20.2 reduce-scatter.12
  338.4 38.4 reduce-scatter.10
  403.8 22.2 reduce-scatter.14
  473.8 38.5 reduce-scatter.16
